TPU v7x, 32 devices: a whole 2x2x4 slice. The times are simulated.
32 devices in a mesh: group: 2 (over y), tm: 4 (over z), seq: 2 (over x), mp: 2 (over core).
Axes of the slice: x: 2, y: 2, z: 4, core: 2. Of those that a mesh axis runs over, the one named last changes fastest.
Arguments:
- states: bfloat16 [8, 128, 5120], P(('group', 'tm'), 'seq'), parts along dimension 0, may hold values from -6 to 6
- start_step: int32 [2], P('group'), parts along dimension 0, may hold values from 0 to 96
- w_qkv: bfloat16 [3, 5120, 3072], P(None, 'tm', ('seq', 'mp')), may hold values from -0.078125 to 0.078125
- qk_gain: float32 [2, 3072], P(None, ('seq', 'mp')), may hold values from 0.25 to 1.75
- w_out: bfloat16 [5120, 3072], P('tm', ('seq', 'mp')), may hold values from -0.109375 to 0.109375
- time_proj: bfloat16 [256, 15360], P('tm'), may hold values from -0.375 to 0.375
Outputs:
- displacement: float32 [8, 128, 5120], P(('group', 'tm'), 'seq', 'mp'), parts along dimension 0
There are 2 independent parts, one for each index of `group`. A program takes and returns all parts, laid end to end along the dimension named above; an argument that names none is the same for every part. Nothing has to cross between parts.
Inputs may be any that keep to these rules, and one draw needn't show every extreme that they name: `start_step`: the window lies inside the trajectory.
All inputs are finite; a program needn't handle non-finite values.
Results may differ from a plain program's by a relative error of at most 0.0029.
Values may be sent and summed in bfloat16 or wider, within the bound.
No kernel may reach another device: no remote copies, remote signals or barrier semaphores. Data moves between devices by JAX's collectives and lax.ppermute only.
A program may use at most 128 MiB of HBM per device.

v0:
```python
import jax
import jax.numpy as jnp
from jax import lax
from jax.sharding import PartitionSpec as P

HEAD_DIM = 128
FREQ = 256
STEPS = 100
sample_shift = 5.0
norm_eps = 1e-06


def from_behind(block, axis, distance):
    devices = range(lax.axis_size(axis))
    route = [(i - distance, i) for i in devices if i - distance in devices]
    return lax.ppermute(block, axis, route)


def sigma_of(index):
    unit = 1.0 - index.astype(jnp.float32) / jnp.float32(STEPS)
    return sample_shift * unit / (1.0 + (sample_shift - 1.0) * unit)


def embed_time(sigma_now):
    half_freq = FREQ // 2
    ranks = jnp.arange(half_freq).astype(jnp.float32)
    freqs = jnp.exp(-jnp.log(jnp.float32(10000.0)) * ranks / jnp.float32(half_freq))
    angles = (1000.0 * sigma_now)[:, None] * freqs[None, :]
    return jnp.concatenate([jnp.cos(angles), jnp.sin(angles)], axis=1).astype(jnp.bfloat16)


def head_norm(values, gain, frames, seq_len, heads_dev):
    shaped = values.reshape(frames, seq_len, heads_dev, HEAD_DIM)
    meansq = jnp.mean(shaped * shaped, axis=-1, keepdims=True)
    scaled = shaped * lax.rsqrt(meansq + norm_eps) * gain.reshape(heads_dev, HEAD_DIM)
    return scaled.astype(jnp.bfloat16)


def attend(query, keys, values):
    frames, seq_len, heads_dev, head_size = query.shape
    block = min(seq_len, 512)
    blocks = seq_len // block
    inv_root = 1.0 / jnp.sqrt(jnp.float32(head_size))
    stacked = query.reshape(frames, blocks, block, heads_dev, head_size).transpose(1, 0, 2, 3, 4)

    def one_block(q_block):
        scores = (
            jnp.einsum("wqhd,wkhd->whqk", q_block, keys, preferred_element_type=jnp.float32)
            * inv_root
        )
        expo = jnp.exp(scores)
        probs = (expo / jnp.sum(expo, axis=-1, keepdims=True)).astype(jnp.bfloat16)
        return jnp.einsum(
            "whqk,wkhd->wqhd", probs, values, preferred_element_type=jnp.float32
        ).astype(jnp.bfloat16)

    result = lax.map(one_block, stacked)
    return result.transpose(1, 0, 2, 3, 4).reshape(frames, seq_len, heads_dev * head_size)


def on_device(states, start_step, w_qkv, qk_gain, w_out, time_proj):
    frames, tok, width = states.shape
    n_tm = lax.axis_size("tm")
    n_mp = lax.axis_size("mp")
    window = frames * n_tm
    tm_pos = lax.axis_index("tm")
    steps_idx = start_step[0] + jnp.arange(window)
    sigma_now = sigma_of(steps_idx)
    step_size = sigma_of(steps_idx + 1) - sigma_now
    emb = embed_time(sigma_now)
    freq_rows = time_proj.shape[0]
    emb_cols = lax.dynamic_slice_in_dim(emb, tm_pos * freq_rows, freq_rows, 1)
    modulation = lax.psum_scatter(
        jnp.dot(emb_cols, time_proj, preferred_element_type=jnp.float32),
        "tm",
        scatter_dimension=0,
        tiled=True,
    )
    shift = modulation[:, :width]
    scale = modulation[:, width : 2 * width]
    gate = modulation[:, 2 * width :]
    field = states.astype(jnp.float32)
    mean = jnp.mean(field, axis=-1, keepdims=True)
    centred = field - mean
    var = jnp.mean(centred * centred, axis=-1, keepdims=True)
    normed = centred * lax.rsqrt(var + norm_eps)
    hidden = (normed * (1.0 + scale[:, None, :]) + shift[:, None, :]).astype(jnp.bfloat16)
    whole = lax.all_gather(hidden, "seq", axis=1, tiled=True)
    seq_len = whole.shape[1]
    flat = whole.reshape(frames * seq_len, width)
    head_cols = w_qkv.shape[2]
    heads_dev = head_cols // HEAD_DIM
    proj = jnp.einsum(
        "rd,cdh->crh",
        flat,
        lax.all_gather(w_qkv, "tm", axis=1, tiled=True),
        preferred_element_type=jnp.float32,
    )
    query = head_norm(proj[0], qk_gain[0], frames, seq_len, heads_dev)
    keys = head_norm(proj[1], qk_gain[1], frames, seq_len, heads_dev)
    values = proj[2].astype(jnp.bfloat16).reshape(frames, seq_len, heads_dev, HEAD_DIM)
    attn = attend(query, keys, values)
    out_full = lax.all_gather(w_out, "tm", axis=0, tiled=True)
    half_width = width // n_mp
    rows = frames * tok
    first = jnp.int32(0) // rows
    pieces = []
    for offset in range(rows * lax.axis_size(("seq", "mp")) // rows):
        owner = first + offset
        segment = owner // n_mp
        column = owner % n_mp
        tokens_part = lax.dynamic_slice_in_dim(attn, segment * tok, tok, 1)
        weight_part = lax.dynamic_slice_in_dim(out_full, column * half_width, half_width, 0)
        product = jnp.einsum(
            "tsh,eh->tse", tokens_part, weight_part, preferred_element_type=jnp.float32
        )
        pieces.append(product.reshape(rows, half_width))
    out_part = lax.psum_scatter(
        jnp.concatenate(pieces, axis=0), ("seq", "mp"), scatter_dimension=0, tiled=True
    ).reshape(frames, tok, half_width)
    gate_own = lax.dynamic_slice_in_dim(gate, lax.axis_index("mp") * half_width, half_width, 1)
    own_steps = lax.dynamic_slice_in_dim(step_size, tm_pos * frames, frames, 0)
    drift = gate_own[:, None, :] * out_part
    increments = own_steps[:, None, None] * drift
    local_sums = jnp.cumsum(increments, axis=0)
    block_total = local_sums[-1]
    running = block_total
    for level in range((n_tm - 1).bit_length()):
        running = running + from_behind(running, "tm", 1 << level)
    before = running - block_total
    return before[None, :, :] + local_sums


def solution(mesh):
    return jax.shard_map(
        on_device,
        mesh=mesh,
        in_specs=(
            P(("group", "tm"), "seq", None),
            P("group"),
            P(None, "tm", ("seq", "mp")),
            P(None, ("seq", "mp")),
            P("tm", ("seq", "mp")),
            P("tm", None),
        ),
        out_specs=P(("group", "tm"), "seq", "mp"),
        check_vma=False,
    )
```

profile of v0, /device:TPU:25, one launch (start us, length us, event | category | flops | bytes accessed | tf_op | source)
XLA Modules:
  0.0 721.7 jit_solution(13477119722304982495)
XLA Ops:
  7.4 0.5 divide_subtract_fusion
  7.9 0.1 fusion.24
  8.0 0.3 copy-done
  8.3 1.1 fusion.26
  9.4 0.0 all-reduce.3.cloned.1.call-update
  9.5 0.0 all-gather.4.cloned.1.call-start
  9.5 0.2 convert_reduce_fusion
  9.7 0.3 fusion.10
  10.1 0.6 dynamic-slice.1
  10.7 32.4 %all-reduce.3.cloned.1.call-done = f32[4,15360]{1,0:T(4,128)} async-done(((f32[4,15360]{1,0:T(4,128)}), f32[4,15360]{1,0:T(4,128)}) %all-reduce.3.cloned.1.call-update) | async-done | bytes 245776
  43.0 1.7 dynamic-slice_add_fusion
  44.7 1.1 fusion.13
  45.8 0.0 all-gather.4.cloned.1.call-update
  45.9 0.0 all-gather.6.cloned.1.call-start
  45.9 0.7 all-gather.6.cloned.1.call-update
  46.6 0.0 all-gather.8.cloned.1.call-start
  46.7 0.5 all-gather.8.cloned.1.call-update
  47.2 0.0 reduce-scatter.2.cloned.1.call-start
  47.3 25.9 %all-gather.4.cloned.1.call-done = bf16[1,128,5120]{2,1,0:T(8,128)(2,1)} async-done(((bf16[1,64,5120]{2,1,0:T(8,128)(2,1)}), bf16[1,128,5120]{2,1,0:T(8,128)(2,1)}) %all-gather.4.cloned.1.call-update) | async-done | bytes 1310736 | tf_op jit(solution)/shard_map/all_gather | solution.py:88
  73.2 398.3 %all-gather.6.cloned.1.call-done = bf16[3,5120,768]{2,1,0:T(8,128)(2,1)} async-done(((bf16[3,1280,768]{2,1,0:T(8,128)(2,1)}), bf16[3,5120,768]{2,1,0:T(8,128)(2,1)}) %all-gather.6.cloned.1.call-update) | async-done | bytes 23592976 | tf_op jit(solution)/shard_map/all_gather | solution.py:96
  471.4 10.0 %convolution_bitcast_fusion = f32[3,128,768]{2,1,0:T(8,128)S(1)} fusion(bf16[3,5120,768]{2,1,0:T(8,128)(2,1)} %all-gather.6.cloned.1.call-done, bf16[1,128,5120]{2,1,0:T(8,128)(2,1)} %all-gather.4.cloned.1.call-done), kind=kOutput, calls=%fused_computation.13 | convolution fusion | flops 3019898880 | bytes 26083328 | tf_op jit(solution)/shard_map/rd,cdh->crh/dot_general | solution.py:93
  481.4 0.7 slice.45
  482.1 0.1 slice_multiply_fusion.1
  482.3 0.9 copy.23
  483.2 0.2 copy.21
  483.3 1.1 reduce_sum.49
  484.5 0.2 copy.22
  484.6 0.2 copy.20
  484.8 1.1 copy.19
  485.9 0.5 fusion.15
  486.4 0.2 convolution_convert_fusion
  486.7 125.4 %all-gather.8.cloned.1.call-done = bf16[5120,768]{1,0:T(8,128)(2,1)} async-done(((bf16[1280,768]{1,0:T(8,128)(2,1)}), bf16[5120,768]{1,0:T(8,128)(2,1)}) %all-gather.8.cloned.1.call-update) | async-done | bytes 7864336 | tf_op jit(solution)/shard_map/all_gather | solution.py:103
  612.1 3.6 fusion.2
  615.7 3.6 fusion.4
  619.3 1.3 fusion.6
  620.6 1.5 fusion
  622.1 1.7 pad_maximum_fusion
  623.8 0.6 copy-done.5
  624.3 0.6 dynamic_slice.28
  624.9 1.5 dynamic-slice_reduce_fusion
  626.4 32.9 %reduce-scatter.2.cloned.1.call-done = f32[64,2560]{1,0:T(8,128)} async-done(((f32[256,2560]{1,0:T(8,128)}), f32[64,2560]{1,0:T(8,128)}) %reduce-scatter.2.cloned.1.call-update) | async-done | bytes 655376 | tf_op jit(solution)/shard_map/reduce_scatter | solution.py:118
  659.4 1.8 multiply_multiply_fusion
  661.1 1.3 collective-permute-start
  662.4 16.1 %collective-permute-done = f32[64,2560]{1,0:T(8,128)S(1)} collective-permute-done((f32[64,2560]{1,0:T(8,128)S(1)}, f32[64,2560]{1,0:T(8,128)S(1)}, u32[]{:S(2)}, u32[]{:S(2)}) %collective-permute-start) | collective-permute-done | bytes 655392 | tf_op jit(solution)/shard_map/ppermute | solution.py:16
  678.5 1.7 fusion.35
  680.2 1.3 collective-permute-start.1
  681.5 32.1 %collective-permute-done.1 = f32[64,2560]{1,0:T(8,128)S(1)} collective-permute-done((f32[64,2560]{1,0:T(8,128)S(1)}, f32[64,2560]{1,0:T(8,128)S(1)}, u32[]{:S(2)}, u32[]{:S(2)}) %collective-permute-start.1) | collective-permute-done | bytes 655392 | tf_op jit(solution)/shard_map/ppermute | solution.py:16
  713.7 1.5 fusion.16
  (21 shorter events, 0.1 us)
Async XLA Ops:
  6.5 1.8 copy-start
  6.5 3.5 copy-start.6
  6.5 3.0 copy-start.2
  6.5 36.5 %all-reduce.3.cloned.1.call-start = ((), (), s32[]{:S(2)}) async-start(), calls=%async_computation.5 | async-start | bytes 491520
  9.5 63.7 %all-gather.4.cloned.1.call-start = ((), (), s32[]{:S(2)}) async-start(), calls=%async_computation.1 | async-start | bytes 1966080 | tf_op jit(solution)/shard_map/all_gather | solution.py:88
  45.9 1.4 copy-start.4
  45.9 425.6 %all-gather.6.cloned.1.call-start = ((), (), s32[]{:S(2)}) async-start(), calls=%async_computation.2 | async-start | bytes 29491200 | tf_op jit(solution)/shard_map/all_gather | solution.py:96
  46.6 565.5 %all-gather.8.cloned.1.call-start = ((), (), s32[]{:S(2)}) async-start(), calls=%async_computation.3 | async-start | bytes 9830400 | tf_op jit(solution)/shard_map/all_gather | solution.py:103
  47.2 612.2 %reduce-scatter.2.cloned.1.call-start = ((), (), s32[]{:S(2)}) async-start(), calls=%async_computation.4 | async-start | bytes 3276800 | tf_op jit(solution)/shard_map/reduce_scatter | solution.py:118
  612.1 7.1 copy-start.1
  623.8 0.6 copy-start.5
  659.4 54.3 %copy-start.3 = (f32[64,2560]{1,0:T(8,128)S(1)}, f32[64,2560]{1,0:T(8,128)}, u32[]{:S(2)}) copy-start(f32[64,2560]{1,0:T(8,128)} %reduce-scatter.2.cloned.1.call-done) | copy-start | bytes 1966084
  661.1 17.4 %collective-permute-start = (f32[64,2560]{1,0:T(8,128)S(1)}, f32[64,2560]{1,0:T(8,128)S(1)}, u32[]{:S(2)}, u32[]{:S(2)}) collective-permute-start(f32[64,2560]{1,0:T(8,128)S(1)} %multiply_multiply_fusion), channel_id=1, source_target_pairs={{0,4},{4,8},{8,12},{1,5},{5,9},{9,13},{2,6},{6,10},{10,14},{3,7},{... | collective-permute-start | bytes 1966088 | tf_op jit(solution)/shard_map/ppermute | solution.py:16
  680.2 33.4 %collective-permute-start.1 = (f32[64,2560]{1,0:T(8,128)S(1)}, f32[64,2560]{1,0:T(8,128)S(1)}, u32[]{:S(2)}, u32[]{:S(2)}) collective-permute-start(f32[64,2560]{1,0:T(8,128)S(1)} %fusion.35), channel_id=1, source_target_pairs={{0,8},{4,12},{1,9},{5,13},{2,10},{6,14},{3,11},{7,15},{16,24},{20,... | collective-permute-start | bytes 1966088 | tf_op jit(solution)/shard_map/ppermute | solution.py:16
Sparse Core Ops, SparseCore 0:
  9.7 33.3 all-reduce.2
  46.0 27.1 all-gather.3
  74.7 396.6 all-gather.5
  472.9 139.2 all-gather.7
  623.9 35.4 reduce-scatter.1
where the time goes:
time: 722 us
  waiting for transfers between devices  664 us (92%)
  matrix products  21.8 us (3%)
  between operations  14.1 us (2%)
  other arithmetic  12 us (2%)
    all_gather x1, waiting for transfers between devices, on_device(): lax.all_gather(w_qkv, 'tm', axis=1, tiled=True)  398 us
    all_gather x1, waiting for transfers between devices, on_device(): out_full = lax.all_gather(w_out, 'tm', axis=0, tiled=True)  125 us
    ppermute x2, waiting for transfers between devices, from_behind(): return lax.ppermute(block, axis, route)  48.2 us
    unnamed x6, waiting for transfers between devices  33.6 us
    reduce_scatter x1, waiting for transfers between devices, on_device(): lax.psum_scatter(jnp.concatenate(pieces, axis=0), ('seq', 'mp'), scatter_...  32.9 us
    all_gather x1, waiting for transfers between devices, on_device(): whole = lax.all_gather(hidden, 'seq', axis=1, tiled=True)  25.9 us
  transfers between devices with their start and end apart: 7, of which 7 were waited for; matrix products, arithmetic and copies ran while one was open for 3% of the time, Pallas kernels for 0%

commit v1 on v0

--- a/solution.py
+++ b/solution.py
@@ -59,6 +59,21 @@
 
 
 def on_device(states, start_step, w_qkv, qk_gain, w_out, time_proj):
+
+    def tiles_fit(matrix, base_x):
+        along_axis = "tm"
+        local_now, tmp = (lax.psum(1, along_axis), lax.axis_index(along_axis))
+        mixed_arr = range(local_now)
+        t_next = map(lambda it: (it, (it - 1) % local_now), mixed_arr)
+        found = list(t_next)
+        value_now = matrix.shape[1]
+        aux = matrix
+        part_now = base_x(aux, tmp * value_now)
+        for p in tuple(range(1, local_now)):
+            aux = lax.ppermute(aux, along_axis, found)
+            part_now = part_now + base_x(aux, (tmp + p) % local_now * value_now)
+        return part_now
+
     frames, tok, width = states.shape
     n_tm = lax.axis_size("tm")
     n_mp = lax.axis_size("mp")
@@ -90,11 +105,14 @@
     flat = whole.reshape(frames * seq_len, width)
     head_cols = w_qkv.shape[2]
     heads_dev = head_cols // HEAD_DIM
-    proj = jnp.einsum(
-        "rd,cdh->crh",
-        flat,
-        lax.all_gather(w_qkv, "tm", axis=1, tiled=True),
-        preferred_element_type=jnp.float32,
+    proj = tiles_fit(
+        w_qkv,
+        lambda own_block, start: jnp.einsum(
+            "rd,cdh->crh",
+            lax.dynamic_slice_in_dim(flat, start, own_block.shape[1], axis=1),
+            own_block,
+            preferred_element_type=jnp.float32,
+        ),
     )
     query = head_norm(proj[0], qk_gain[0], frames, seq_len, heads_dev)
     keys = head_norm(proj[1], qk_gain[1], frames, seq_len, heads_dev)

time: 722 us -> 664 us (0.920)
  waiting for transfers between devices: 664 us -> 561 us
  starting transfers between devices: 2.75 us -> 42.8 us
    all_gather x1 -> x0, waiting for transfers between devices: 398 us -> none  [on_device(): lax.all_gather(w_qkv, 'tm', axis=1, tiled=True)]
    ppermute x0 -> x3, waiting for transfers between devices: none -> 330 us  [tiles_fit(): aux = lax.ppermute(aux, along_axis, found)]
    all_gather x1, waiting for transfers between devices: 125 us -> 0.02 us  [on_device(): out_full = lax.all_gather(w_out, 'tm', axis=0, tiled=True)]
    unnamed x6 -> x5, waiting for transfers between devices: 33.6 us -> 150 us
    ppermute x0 -> x3, starting transfers between devices: none -> 40.1 us  [tiles_fit(): aux = lax.ppermute(aux, along_axis, found)]
    all_gather x1, waiting for transfers between devices: 25.9 us -> 0.02 us  [on_device(): whole = lax.all_gather(hidden, 'seq', axis=1, tiled=True)]
    dot_general x1 -> x4, matrix products: 9.97 us -> 14.9 us  [on_device(): jnp.einsum('rd,cdh->crh', lax.dynamic_slice_in_dim(flat, start, own_block...]
  transfers between devices with their start and end apart: 7 -> 9, of which waited for: 7 -> 6; matrix products, arithmetic and copies ran while one was open for 3% -> 4% of each run, Pallas kernels for 0% -> 0%
where the time goes in v1:
time: 664 us
  waiting for transfers between devices  561 us (84%)
  starting transfers between devices  42.8 us (6%)
  matrix products  26.7 us (4%)
  between operations  14.2 us (2%)
  other arithmetic  12.2 us (2%)
    ppermute x3, waiting for transfers between devices, tiles_fit(): aux = lax.ppermute(aux, along_axis, found)  330 us
    unnamed x5, waiting for transfers between devices  150 us
    ppermute x2, waiting for transfers between devices, from_behind(): return lax.ppermute(block, axis, route)  48.2 us
    ppermute x3, starting transfers between devices, tiles_fit(): aux = lax.ppermute(aux, along_axis, found)  40.1 us
    reduce_scatter x1, waiting for transfers between devices, on_device(): lax.psum_scatter(jnp.concatenate(pieces, axis=0), ('seq', 'mp'), scatter_...  33.9 us
    dot_general x4, matrix products, on_device(): jnp.einsum('rd,cdh->crh', lax.dynamic_slice_in_dim(flat, start, own_block...  14.9 us
  transfers between devices with their start and end apart: 9, of which 6 were waited for; matrix products, arithmetic and copies ran while one was open for 4% of the time, Pallas kernels for 0%

profile of v1, /device:TPU:25, one launch (start us, length us, event | category | flops | bytes accessed | tf_op | source)
XLA Modules:
  0.0 663.7 jit_solution(14460496490991614508)
XLA Ops:
  6.5 0.2 collective-permute-start
  7.6 0.6 divide_subtract_fusion
  8.2 0.1 fusion.33
  8.3 1.1 fusion.39
  9.5 0.0 all-gather.3.cloned.1.call-start
  9.5 0.2 convert_reduce_fusion
  9.7 0.3 fusion.11
  10.1 0.6 dynamic-slice.5
  10.7 148.8 %all-reduce.3.cloned.1.call-done = f32[4,15360]{1,0:T(4,128)} async-done(((f32[4,15360]{1,0:T(4,128)}), f32[4,15360]{1,0:T(4,128)}) %all-reduce.3.cloned.1.call-update) | async-done | bytes 245776
  159.5 1.6 dynamic-slice_add_fusion
  161.1 1.2 collective-permute-start.1
  162.3 1.1 fusion.14
  163.5 0.0 all-gather.5.cloned.1.call-start
  163.5 0.7 all-gather.5.cloned.1.call-update
  164.2 0.0 reduce-scatter.2.cloned.1.call-start
  164.2 210.2 %collective-permute-done.1 = bf16[3,1280,768]{2,1,0:T(8,128)(2,1)} collective-permute-done((bf16[3,1280,768]{2,1,0:T(8,128)(2,1)}, bf16[3,1280,768]{2,1,0:T(8,128)(2,1)}, u32[]{:S(2)}, u32[]{:S(2)}) %collective-permute-start.1) | collective-permute-done | bytes 5898272 | tf_op jit(solution)/shard_map/ppermute | solution.py:73
  374.4 38.7 %collective-permute-start.2 = (bf16[3,1280,768]{2,1,0:T(8,128)(2,1)}, bf16[3,1280,768]{2,1,0:T(8,128)(2,1)}, u32[]{:S(2)}, u32[]{:S(2)}) collective-permute-start(bf16[3,1280,768]{2,1,0:T(8,128)(2,1)} %collective-permute-done.1), channel_id=1, source_target_pairs={{0,12},{4,0},{8,4},{12,8},{1,13},{5,1},{9,5},{13,9},{2,14},{6,2},{... | collective-permute-start | bytes 17694728 | tf_op jit(solution)/shard_map/ppermute | solution.py:73
  413.2 3.8 fusion.20
  417.0 3.7 convolution_add_fusion.2
  420.7 3.7 convolution_add_fusion.1
  424.4 119.4 %collective-permute-done.2 = bf16[3,1280,768]{2,1,0:T(8,128)(2,1)} collective-permute-done((bf16[3,1280,768]{2,1,0:T(8,128)(2,1)}, bf16[3,1280,768]{2,1,0:T(8,128)(2,1)}, u32[]{:S(2)}, u32[]{:S(2)}) %collective-permute-start.2) | collective-permute-done | bytes 5898272 | tf_op jit(solution)/shard_map/ppermute | solution.py:73
  543.9 3.7 fusion.10
  547.6 0.7 slice.45
  548.3 0.1 slice_multiply_fusion.1
  548.4 0.9 copy.23
  549.3 0.2 copy.21
  549.5 1.0 reduce_sum.49
  550.5 0.2 copy.20
  550.7 0.2 copy.22
  550.9 1.1 copy.19
  552.0 0.5 fusion.15
  552.5 0.2 convolution_convert_fusion
  552.8 3.6 fusion.2
  556.4 3.6 fusion.4
  559.9 1.3 fusion.6
  561.2 1.5 fusion
  562.7 1.7 pad_maximum_fusion
  564.5 0.6 copy-done.6
  565.1 0.6 dynamic_slice.48
  565.7 1.4 dynamic-slice_reduce_fusion
  567.2 33.9 %reduce-scatter.2.cloned.1.call-done = f32[64,2560]{1,0:T(8,128)} async-done(((f32[256,2560]{1,0:T(8,128)}), f32[64,2560]{1,0:T(8,128)}) %reduce-scatter.2.cloned.1.call-update) | async-done | bytes 655376 | tf_op jit(solution)/shard_map/reduce_scatter | solution.py:136
  601.1 1.8 multiply_multiply_fusion
  602.9 1.3 collective-permute-start.3
  604.2 16.1 %collective-permute-done.3 = f32[64,2560]{1,0:T(8,128)S(1)} collective-permute-done((f32[64,2560]{1,0:T(8,128)S(1)}, f32[64,2560]{1,0:T(8,128)S(1)}, u32[]{:S(2)}, u32[]{:S(2)}) %collective-permute-start.3) | collective-permute-done | bytes 655392 | tf_op jit(solution)/shard_map/ppermute | solution.py:16
  620.3 1.8 fusion.50
  622.1 1.3 collective-permute-start.4
  623.4 32.2 %collective-permute-done.4 = f32[64,2560]{1,0:T(8,128)S(1)} collective-permute-done((f32[64,2560]{1,0:T(8,128)S(1)}, f32[64,2560]{1,0:T(8,128)S(1)}, u32[]{:S(2)}, u32[]{:S(2)}) %collective-permute-start.4) | collective-permute-done | bytes 655392 | tf_op jit(solution)/shard_map/ppermute | solution.py:16
  655.6 1.6 fusion.16
  (29 shorter events, 0.2 us)
Async XLA Ops:
  6.5 1.8 copy-start
  6.5 3.6 copy-start.7
  6.5 3.0 copy-start.2
  6.5 152.9 %all-reduce.3.cloned.1.call-start = ((), (), s32[]{:S(2)}) async-start(), calls=%async_computation.4 | async-start | bytes 491520
  6.5 154.5 %collective-permute-start = (bf16[3,1280,768]{2,1,0:T(8,128)(2,1)}, bf16[3,1280,768]{2,1,0:T(8,128)(2,1)}, u32[]{:S(2)}, u32[]{:S(2)}) collective-permute-start(bf16[3,1280,768]{2,1,0:T(8,128)(2,1)} %param.8), channel_id=1, source_target_pairs={{0,12},{4,0},{8,4},{12,8},{1,13},{5,1},{9,5},{13,9},{2,14},{6,2},{... | collective-permute-start | bytes 17694728 | tf_op jit(solution)/shard_map/ppermute | solution.py:73
  9.5 403.7 %all-gather.3.cloned.1.call-start = ((), (), s32[]{:S(2)}) async-start(), calls=%async_computation.1 | async-start | bytes 1966080 | tf_op jit(solution)/shard_map/all_gather | solution.py:103
  161.1 213.3 %collective-permute-start.1 = (bf16[3,1280,768]{2,1,0:T(8,128)(2,1)}, bf16[3,1280,768]{2,1,0:T(8,128)(2,1)}, u32[]{:S(2)}, u32[]{:S(2)}) collective-permute-start(bf16[3,1280,768]{2,1,0:T(8,128)(2,1)} %collective-permute-done), channel_id=1, source_target_pairs={{0,12},{4,0},{8,4},{12,8},{1,13},{5,1},{9,5},{13,9},{2,14},{6,2},{... | collective-permute-start | bytes 17694728 | tf_op jit(solution)/shard_map/ppermute | solution.py:73
  162.3 250.8 %copy-start.5 = (f32[2,768]{1,0:T(2,128)S(1)}, f32[2,768]{1,0:T(2,128)}, u32[]{:S(2)}) copy-start(f32[2,768]{1,0:T(2,128)} %param.9) | copy-start | bytes 18436
  163.5 389.3 %all-gather.5.cloned.1.call-start = ((), (), s32[]{:S(2)}) async-start(), calls=%async_computation.2 | async-start | bytes 9830400 | tf_op jit(solution)/shard_map/all_gather | solution.py:121
  164.2 436.9 %reduce-scatter.2.cloned.1.call-start = ((), (), s32[]{:S(2)}) async-start(), calls=%async_computation.3 | async-start | bytes 3276800 | tf_op jit(solution)/shard_map/reduce_scatter | solution.py:136
  374.4 169.5 %collective-permute-start.2 = (bf16[3,1280,768]{2,1,0:T(8,128)(2,1)}, bf16[3,1280,768]{2,1,0:T(8,128)(2,1)}, u32[]{:S(2)}, u32[]{:S(2)}) collective-permute-start(bf16[3,1280,768]{2,1,0:T(8,128)(2,1)} %collective-permute-done.1), channel_id=1, source_target_pairs={{0,12},{4,0},{8,4},{12,8},{1,13},{5,1},{9,5},{13,9},{2,14},{6,2},{... | collective-permute-start | bytes 17694728 | tf_op jit(solution)/shard_map/ppermute | solution.py:73
  413.2 3.8 copy-start.4
  552.8 7.2 %copy-start.1 = (bf16[5120,768]{1,0:T(8,128)(2,1)S(1)}, bf16[5120,768]{1,0:T(8,128)(2,1)}, u32[]{:S(2)}) copy-start(bf16[5120,768]{1,0:T(8,128)(2,1)} %all-gather.5.cloned.1.call-done) | copy-start | bytes 23592964
  564.4 0.7 copy-start.6
  601.1 54.5 %copy-start.3 = (f32[64,2560]{1,0:T(8,128)S(1)}, f32[64,2560]{1,0:T(8,128)}, u32[]{:S(2)}) copy-start(f32[64,2560]{1,0:T(8,128)} %reduce-scatter.2.cloned.1.call-done) | copy-start | bytes 1966084
  602.9 17.4 %collective-permute-start.3 = (f32[64,2560]{1,0:T(8,128)S(1)}, f32[64,2560]{1,0:T(8,128)S(1)}, u32[]{:S(2)}, u32[]{:S(2)}) collective-permute-start(f32[64,2560]{1,0:T(8,128)S(1)} %multiply_multiply_fusion), channel_id=1, source_target_pairs={{0,4},{4,8},{8,12},{1,5},{5,9},{9,13},{2,6},{6,10},{10,14},{3,7},{... | collective-permute-start | bytes 1966088 | tf_op jit(solution)/shard_map/ppermute | solution.py:16
  622.1 33.5 %collective-permute-start.4 = (f32[64,2560]{1,0:T(8,128)S(1)}, f32[64,2560]{1,0:T(8,128)S(1)}, u32[]{:S(2)}, u32[]{:S(2)}) collective-permute-start(f32[64,2560]{1,0:T(8,128)S(1)} %fusion.50), channel_id=1, source_target_pairs={{0,8},{4,12},{1,9},{5,13},{2,10},{6,14},{3,11},{7,15},{16,24},{20,... | collective-permute-start | bytes 1966088 | tf_op jit(solution)/shard_map/ppermute | solution.py:16
Sparse Core Ops, SparseCore 0:
  9.7 149.7 all-reduce.2
  163.6 27.2 all-gather.2
  192.5 227.4 all-gather.4
  564.6 36.4 reduce-scatter.1
